TPU v7x, 256 devices: a whole 4x4x8 slice. The times are simulated.
256 devices in a mesh: slab: 8 (over z), front: 32 (over y, x, core).
Axes of the slice: x: 4, y: 4, z: 8, core: 2. Of those that a mesh axis runs over, the one named last changes fastest.
Arguments:
- leaf_rhs: bfloat16 [8, 2, 512, 128, 512], P('slab', None, 'front'), may hold values from -6 to 6
- leaf_inv: bfloat16 [8, 512, 2, 128, 128], P('slab', 'front'), may hold values from -0.375 to 0.375
- leaf_off: bfloat16 [8, 512, 2, 128, 128], P('slab', 'front'), may hold values from -0.125 to 0.125
- parent: int32 [8, 512, 1], P('slab', 'front'), may hold values from 0 to 31; in each aligned block of 16 rows (0 to 15, 16 to 31, ..., all dimensions but the last counted through in order) no two rows name the same one
- ancestors: int32 [8, 512, 128], P('slab', 'front'), may hold values from 0 to 255
- root_rhs: bfloat16 [8, 2, 8192, 512], P('slab', None, 'front'), may hold values from -6 to 6
- root_inv: float32 [8, 64, 2, 128, 128], P('slab', 'front'), may hold values from -2 to 2.5
- coupling: float32 [8, 8192], P('slab', 'front'), may hold values from 0.6 to 1.3
Outputs:
- leaf_sol: bfloat16 [8, 2, 512, 128, 512], P('slab', None, 'front')
- root_sol: float32 [8, 2, 8192, 512], P('slab', None, 'front')
Inputs may be any that keep to these rules, and one draw needn't show every extreme that they name: Each front index's 16 leaf blocks of a slab name any one parent at most 1 times. `ancestors`: rows may repeat within a block.
All inputs are finite; a program needn't handle non-finite values.
Results may differ from a plain program's by a relative error of at most 0.0057.
Values may be sent and summed in bfloat16 or wider, within the bound.
A program may use at most 128 MiB of HBM per device.

v0:
```python
import jax
import jax.numpy as jnp
from jax import lax
from jax.sharding import PartitionSpec as P


def passed_along(x, axis, by):
    count = lax.axis_size(axis)
    pairs = [(i, i + by) for i in range(count) if 0 <= i + by < count]
    return lax.ppermute(x, axis, pairs)


def planes_apply(real_mat, imag_mat, real_vec, imag_vec, form):
    real = jnp.einsum(form, real_mat, real_vec, preferred_element_type=jnp.float32) - jnp.einsum(
        form, imag_mat, imag_vec, preferred_element_type=jnp.float32
    )
    imag = jnp.einsum(form, real_mat, imag_vec, preferred_element_type=jnp.float32) + jnp.einsum(
        form, imag_mat, real_vec, preferred_element_type=jnp.float32
    )
    return jnp.stack([real, imag])


def block_solve(blocks, field):
    highest = lax.Precision.HIGHEST
    shaped = field.reshape(2, blocks.shape[0], blocks.shape[2], field.shape[-1])
    real = jnp.einsum("kij,kjc->kic", blocks[:, 0], shaped[0], precision=highest) - jnp.einsum(
        "kij,kjc->kic", blocks[:, 1], shaped[1], precision=highest
    )
    imag = jnp.einsum("kij,kjc->kic", blocks[:, 0], shaped[1], precision=highest) + jnp.einsum(
        "kij,kjc->kic", blocks[:, 1], shaped[0], precision=highest
    )
    return jnp.stack([real, imag]).reshape(field.shape)


def body(leaf_rhs, leaf_inv, leaf_off, parent, ancestors, root_rhs, root_inv, coupling):
    forward_form = "lij,ljc->lic"
    back_form = "lji,ljc->lic"
    rhs = leaf_rhs[0]
    inverse = leaf_inv[0]
    offdiag = leaf_off[0]
    owners = parent[0, :, 0]
    anc_rows = ancestors[0]
    fronts = lax.axis_size("front")
    count = owners.shape[0]
    per_owner = (count + fronts - 1) // fronts
    blk = rhs.shape[2]
    width = rhs.shape[3]
    root_rows = root_rhs.shape[2]
    slot_total = fronts * per_owner
    hits = (owners[:, None] == jnp.arange(fronts, dtype=jnp.int32)[None, :]).astype(jnp.int32)
    rank = jnp.sum((jnp.cumsum(hits, axis=0) - hits) * hits, axis=1)
    slot = owners * per_owner + rank
    place_int = (slot[:, None] == jnp.arange(slot_total, dtype=jnp.int32)[None, :]).astype(
        jnp.int32
    )
    place = place_int.astype(jnp.bfloat16)
    slot_ids = jnp.sum(place_int[:, :, None] * anc_rows[:, None, :], axis=0).reshape(
        1, fronts, per_owner, blk
    )
    forward = planes_apply(inverse[:, 0], inverse[:, 1], rhs[0], rhs[1], forward_form).astype(
        jnp.bfloat16
    )
    partial_value = planes_apply(
        offdiag[:, 0], offdiag[:, 1], forward[0], forward[1], forward_form
    ).astype(jnp.bfloat16)
    placed = jnp.einsum(
        "ks,pkbc->psbc", place, partial_value, preferred_element_type=jnp.float32
    ).astype(jnp.bfloat16)
    placed = placed.reshape(2, fronts, per_owner, blk, width)
    arrived, arrived_ids = (
        lax.all_to_all(placed, "front", split_axis=1, concat_axis=1, tiled=True),
        lax.all_to_all(slot_ids, "front", split_axis=1, concat_axis=1, tiled=True),
    )
    slot_parts = arrived.reshape(2, slot_total * blk, width)
    flat_ids = arrived_ids.reshape(-1)
    row_table = (flat_ids[:, None] == jnp.arange(root_rows, dtype=jnp.int32)[None, :]).astype(
        jnp.bfloat16
    )
    summed = jnp.einsum("sr,psc->prc", row_table, slot_parts, preferred_element_type=jnp.float32)
    reduced = root_rhs[0].astype(jnp.float32) - summed
    blocks = root_inv[0]
    cpl = coupling[0]
    first = block_solve(blocks, reduced)

    def relay(step, state):
        previous = passed_along(state, "slab", 1)
        return block_solve(blocks, reduced - cpl[None, :, None] * previous)

    state = lax.fori_loop(0, lax.axis_size("slab") - 1, relay, first)
    root_half = state.astype(jnp.bfloat16)
    slot_rows = jnp.einsum(
        "sr,prc->psc", row_table, root_half, preferred_element_type=jnp.float32
    ).astype(jnp.bfloat16)
    slot_rows = slot_rows.reshape(2, fronts, per_owner, blk, width)
    returned = lax.all_to_all(slot_rows, "front", split_axis=1, concat_axis=1, tiled=True)
    picked = jnp.einsum(
        "ks,psbc->pkbc",
        place,
        returned.reshape(2, slot_total, blk, width),
        preferred_element_type=jnp.float32,
    ).astype(jnp.bfloat16)
    back = planes_apply(offdiag[:, 0], offdiag[:, 1], picked[0], picked[1], back_form).astype(
        jnp.bfloat16
    )
    solved = forward.astype(jnp.float32) - planes_apply(
        inverse[:, 0], inverse[:, 1], back[0], back[1], forward_form
    )
    return (solved.astype(jnp.bfloat16)[None], state[None])


def solution(mesh):
    in_specs = (
        P("slab", None, "front", None, None),
        P("slab", "front", None, None, None),
        P("slab", "front", None, None, None),
        P("slab", "front", None),
        P("slab", "front", None),
        P("slab", None, "front", None),
        P("slab", "front", None, None, None),
        P("slab", "front"),
    )
    out_specs = (P("slab", None, "front", None, None), P("slab", None, "front", None))
    return jax.shard_map(body, mesh=mesh, in_specs=in_specs, out_specs=out_specs, check_vma=False)
```

profile of v0, /device:TPU:129, one launch (start us, length us, event | category | flops | bytes accessed | tf_op | source)
XLA Modules:
  0.0 566.3 jit_solution(2342361114886660467)
XLA Ops:
  0.6 1.4 copy.117
  2.1 4.8 fusion.20
  6.9 2.7 fusion.24
  10.0 3.9 add_convert_fusion.2
  14.4 1.3 copy-done.10
  16.4 0.8 fusion.45
  17.2 0.8 fusion.46
  18.0 0.9 fusion.33
  18.9 0.9 fusion.32
  19.8 2.4 pad_maximum_fusion.1
  22.2 8.3 %copy.77 = bf16[2,16,128,512]{3,1,2,0:T(8,128)(2,1)} copy(bf16[2,16,128,512]{2,3,1,0:T(8,128)(2,1)} %pad_maximum_fusion.1) | data formatting | bytes 8388608 | tf_op jit(solution)/shard_map/stack | solution.py:20
  30.6 7.9 %convert_bitcast_fusion = bf16[2,32,1,128,512]{4,1,3,0,2:T(8,128)(2,1)} fusion(bf16[2,16,128,512]{3,1,2,0:T(8,128)(2,1)} %copy.77, s32[16]{0:T(128)S(1)} %bitcast_add_fusion), kind=kOutput, calls=%fused_computation.19 | convolution fusion | flops 138413568 | bytes 12582976 | tf_op jit(solution)/shard_map/ks,pkbc->psbc/dot_general | solution.py:66
  38.4 11.4 %copy.78 = bf16[2,32,1,128,512]{4,3,0,2,1:T(8,128)(2,1)} copy(bf16[2,32,1,128,512]{4,1,3,0,2:T(8,128)(2,1)} %convert_bitcast_fusion) | data formatting | bytes 16777216 | tf_op jit(solution)/shard_map/reshape | solution.py:69
  49.8 8.0 %all-to-all-start = ((bf16[2,32,1,128,512]{4,3,0,2,1:T(8,128)(2,1)}), bf16[2,32,1,128,512]{4,3,0,2,1:T(8,128)(2,1)}, u32[]{:S(2)}, u32[]{:S(2)}) async-start(bf16[2,32,1,128,512]{4,3,0,2,1:T(8,128)(2,1)} %copy.78), calls=%async_computation | async-start | bytes 16777216 | tf_op jit(solution)/shard_map/all_to_all | solution.py:71
  57.8 0.7 multiply_reduce_fusion
  58.6 99.9 %all-to-all-done = bf16[2,32,1,128,512]{4,3,0,2,1:T(8,128)(2,1)} async-done(((bf16[2,32,1,128,512]{4,3,0,2,1:T(8,128)(2,1)}), bf16[2,32,1,128,512]{4,3,0,2,1:T(8,128)(2,1)}, u32[]{:S(2)}, u32[]{:S(2)}) %all-to-all-start) | async-done | bytes 8388640 | tf_op jit(solution)/shard_map/all_to_all | solution.py:71
  158.4 9.2 %all-to-all-start.1 = ((s32[1,32,1,128]{3,2,0,1:T(1,128)}), s32[1,32,1,128]{3,2,0,1:T(1,128)S(1)}, u32[]{:S(2)}, u32[]{:S(2)}) async-start(s32[1,32,1,128]{3,2,0,1:T(1,128)} %bitcast.32), calls=%async_computation.1 | async-start | bytes 32768 | tf_op jit(solution)/shard_map/all_to_all | solution.py:72
  167.7 7.6 %copy.79 = bf16[2,32,1,128,512]{4,3,1,0,2:T(8,128)(2,1)} copy(bf16[2,32,1,128,512]{4,3,0,2,1:T(8,128)(2,1)} %all-to-all-done) | data formatting | bytes 16777216 | tf_op jit(solution)/shard_map/all_to_all | solution.py:71
  175.3 6.7 %fusion.37 = f32[2,256,512]{2,1,0:T(8,128)S(1)} fusion(bf16[2,4096,512]{2,1,0:T(8,128)(2,1)} %bitcast.229, s32[4096]{0:T(1024)S(1)} %bitcast.237, bf16[1,2,256,512]{3,2,1,0:T(8,128)(2,1)} %param.15), kind=kOutput, calls=%fused_computation.51 | convolution fusion | flops 2149056512 | bytes 9977856 | tf_op jit(solution)/shard_map/sr,psc->prc/dot_general | solution.py:79
  184.5 1.0 pad_maximum_fusion.2
  185.6 212.0 %while.10 = (s32[]{:T(128)}, f32[2,256,512]{2,1,0:T(8,128)}, f32[1,256]{1,0:T(1,128)S(1)}, f32[2,256,512]{2,1,0:T(8,128)S(1)}, f32[2,2,128,128]{3,2,0,1:T(8,128)S(1)}, /*index=5*/s32[]{:T(128)}) while((s32[]{:T(128)}, f32[2,256,512]{2,1,0:T(8,128)}, f32[1,256]{1,0:T(1,128)S(1)}, f32[2,256,512]{2,1,0:T(8,128)S(1)}, ...), condition=%wide.region_4.5_spmd, body=%wide.region_3.4_spmd.sunk | while | flops 806354944 | bytes 17302636 | solution.py:89
  185.6 2.6 collective-permute-start
  188.2 25.3 %collective-permute-done = f32[2,256,512]{2,1,0:T(8,128)} collective-permute-done((f32[2,256,512]{2,1,0:T(8,128)}, f32[2,256,512]{2,1,0:T(8,128)}, u32[]{:S(2)}, u32[]{:S(2)}) %collective-permute-start) | collective-permute-done | bytes 1048608 | tf_op jit(solution)/shard_map/while/body/eval_jaxpr/ppermute | solution.py:10
  213.5 1.4 multiply_subtract_fusion.2
  217.4 1.0 pad_maximum_fusion.4
  218.4 1.9 collective-permute-start
  220.4 25.1 %collective-permute-done = f32[2,256,512]{2,1,0:T(8,128)} collective-permute-done((f32[2,256,512]{2,1,0:T(8,128)}, f32[2,256,512]{2,1,0:T(8,128)}, u32[]{:S(2)}, u32[]{:S(2)}) %collective-permute-start) | collective-permute-done | bytes 1048608 | tf_op jit(solution)/shard_map/while/body/eval_jaxpr/ppermute | solution.py:10
  245.5 1.4 multiply_subtract_fusion.2
  249.4 1.0 pad_maximum_fusion.4
  250.4 1.9 collective-permute-start
  252.4 24.3 %collective-permute-done = f32[2,256,512]{2,1,0:T(8,128)} collective-permute-done((f32[2,256,512]{2,1,0:T(8,128)}, f32[2,256,512]{2,1,0:T(8,128)}, u32[]{:S(2)}, u32[]{:S(2)}) %collective-permute-start) | collective-permute-done | bytes 1048608 | tf_op jit(solution)/shard_map/while/body/eval_jaxpr/ppermute | solution.py:10
  276.6 1.4 multiply_subtract_fusion.2
  280.5 1.0 pad_maximum_fusion.4
  281.6 1.9 collective-permute-start
  283.5 23.4 %collective-permute-done = f32[2,256,512]{2,1,0:T(8,128)} collective-permute-done((f32[2,256,512]{2,1,0:T(8,128)}, f32[2,256,512]{2,1,0:T(8,128)}, u32[]{:S(2)}, u32[]{:S(2)}) %collective-permute-start) | collective-permute-done | bytes 1048608 | tf_op jit(solution)/shard_map/while/body/eval_jaxpr/ppermute | solution.py:10
  306.9 1.4 multiply_subtract_fusion.2
  310.8 1.0 pad_maximum_fusion.4
  311.9 1.9 collective-permute-start
  313.8 22.6 %collective-permute-done = f32[2,256,512]{2,1,0:T(8,128)} collective-permute-done((f32[2,256,512]{2,1,0:T(8,128)}, f32[2,256,512]{2,1,0:T(8,128)}, u32[]{:S(2)}, u32[]{:S(2)}) %collective-permute-start) | collective-permute-done | bytes 1048608 | tf_op jit(solution)/shard_map/while/body/eval_jaxpr/ppermute | solution.py:10
  336.3 1.4 multiply_subtract_fusion.2
  340.3 1.0 pad_maximum_fusion.4
  341.3 1.9 collective-permute-start
  343.2 21.7 %collective-permute-done = f32[2,256,512]{2,1,0:T(8,128)} collective-permute-done((f32[2,256,512]{2,1,0:T(8,128)}, f32[2,256,512]{2,1,0:T(8,128)}, u32[]{:S(2)}, u32[]{:S(2)}) %collective-permute-start) | collective-permute-done | bytes 1048608 | tf_op jit(solution)/shard_map/while/body/eval_jaxpr/ppermute | solution.py:10
  364.9 1.4 multiply_subtract_fusion.2
  368.8 1.0 pad_maximum_fusion.4
  369.9 1.9 collective-permute-start
  371.8 20.8 %collective-permute-done = f32[2,256,512]{2,1,0:T(8,128)} collective-permute-done((f32[2,256,512]{2,1,0:T(8,128)}, f32[2,256,512]{2,1,0:T(8,128)}, u32[]{:S(2)}, u32[]{:S(2)}) %collective-permute-start) | collective-permute-done | bytes 1048608 | tf_op jit(solution)/shard_map/while/body/eval_jaxpr/ppermute | solution.py:10
  392.6 1.4 multiply_subtract_fusion.2
  396.6 1.0 pad_maximum_fusion.4
  397.6 6.7 %convolution_convert_fusion = bf16[2,512,4096]{2,1,0:T(8,128)(2,1)} fusion(s32[4096]{0:T(1024)S(1)} %bitcast.238, f32[2,256,512]{2,1,0:T(8,128)} %get-tuple-element.29), kind=kOutput, calls=%fused_computation.20 | convolution fusion | flops 2152988672 | bytes 9453568 | tf_op jit(solution)/shard_map/sr,prc->psc/dot_general | solution.py:91
  404.3 9.4 %copy.106 = bf16[128,8,32,128]{3,2,1,0:T(8,128)(2,1)} copy(bf16[128,8,32,128]{3,1,2,0:T(8,128)(2,1)} %bitcast.209) | data formatting | bytes 16777216
  413.7 14.0 %copy.84 = bf16[2,32,1,128,512]{4,3,0,2,1:T(8,128)(2,1)} copy(bf16[2,32,1,128,512]{3,1,4,0,2:T(8,128)(2,1)} %bitcast.210) | data formatting | bytes 16777216 | tf_op jit(solution)/shard_map/reshape | solution.py:94
  427.7 108.1 %all_to_all.15 = bf16[2,32,1,128,512]{4,3,0,2,1:T(8,128)(2,1)S(1)} all-to-all(bf16[2,32,1,128,512]{4,3,0,2,1:T(8,128)(2,1)} %copy.84), channel_id=1, replica_groups=mesh['slab'=8,'front'=32] {'front'}, dimensions={1} | all-to-all | bytes 16777216 | tf_op jit(solution)/shard_map/all_to_all | solution.py:95
  535.8 5.9 %convert_bitcast_fusion.1 = bf16[2,16,128,512]{3,1,2,0:T(8,128)(2,1)S(1)} fusion(bf16[2,32,1,128,512]{4,3,0,2,1:T(8,128)(2,1)S(1)} %all_to_all.15, s32[16]{0:T(128)S(1)} %bitcast_add_fusion), kind=kOutput, calls=%fused_computation.26 | convolution fusion | flops 136316416 | bytes 12582976 | tf_op jit(solution)/shard_map/ks,psbc->pkbc/dot_general | solution.py:96
  541.7 2.5 slice_bitcast_fusion.1
  544.2 4.7 copy.86
  548.8 4.5 copy.87
  553.3 2.4 fusion.43
  556.5 0.7 add_convert_fusion
  557.2 0.9 copy-done.6
  558.1 0.7 subtract_convert_fusion
  560.7 0.8 subtract_bitcast_fusion
  562.2 0.9 copy-done.1
  563.1 3.0 fusion.10
  (82 shorter events, 24.9 us)
Async XLA Ops:
  0.6 6.3 %copy-start.8 = (bf16[1,2,16,128,512]{4,3,2,1,0:T(8,128)(2,1)S(1)}, bf16[1,2,16,128,512]{4,3,2,1,0:T(8,128)(2,1)}, u32[]{:S(2)}) copy-start(bf16[1,2,16,128,512]{4,3,2,1,0:T(8,128)(2,1)} %param.10) | copy-start | bytes 12582916
  2.1 11.8 %copy-start.4 = (bf16[1,16,2,128,128]{4,3,1,2,0:T(8,128)(2,1)}, bf16[1,16,2,128,128]{4,3,1,2,0:T(8,128)(2,1)S(1)}, u32[]{:S(2)}) copy-start(bf16[1,16,2,128,128]{4,3,1,2,0:T(8,128)(2,1)S(1)} %copy.117) | copy-start | bytes 3145732
  6.9 2.7 copy-start.15
  6.9 3.0 copy-start.11
  10.0 8.9 %copy-start.2 = (bf16[1,16,2,128,128]{4,3,1,2,0:T(8,128)(2,1)}, bf16[1,16,2,128,128]{4,3,1,2,0:T(8,128)(2,1)S(1)}, u32[]{:S(2)}) copy-start(bf16[1,16,2,128,128]{4,3,1,2,0:T(8,128)(2,1)S(1)} %copy.116) | copy-start | bytes 3145732
  10.0 4.4 copy-start.9
  10.0 5.7 copy-start.10
  16.4 1.6 copy-start
  49.8 8.0 %copy-start.14 = (s32[1,16,128]{2,1,0:T(8,128)S(1)}, s32[1,16,128]{2,1,0:T(8,128)}, u32[]{:S(2)}) copy-start(s32[1,16,128]{2,1,0:T(8,128)} %param.14) | copy-start | bytes 24580
  49.8 117.9 %copy-start.12 = (f32[1,2,2,128,128]{4,3,2,1,0:T(8,128)S(1)}, f32[1,2,2,128,128]{4,3,2,1,0:T(8,128)}, u32[]{:S(2)}) copy-start(f32[1,2,2,128,128]{4,3,2,1,0:T(8,128)} %param.16) | copy-start | bytes 786436
  49.8 108.7 %all-to-all-start = ((bf16[2,32,1,128,512]{4,3,0,2,1:T(8,128)(2,1)}), bf16[2,32,1,128,512]{4,3,0,2,1:T(8,128)(2,1)}, u32[]{:S(2)}, u32[]{:S(2)}) async-start(bf16[2,32,1,128,512]{4,3,0,2,1:T(8,128)(2,1)} %copy.78), calls=%async_computation | async-start | bytes 16777216 | tf_op jit(solution)/shard_map/all_to_all | solution.py:71
  158.4 16.9 %all-to-all-start.1 = ((s32[1,32,1,128]{3,2,0,1:T(1,128)}), s32[1,32,1,128]{3,2,0,1:T(1,128)S(1)}, u32[]{:S(2)}, u32[]{:S(2)}) async-start(s32[1,32,1,128]{3,2,0,1:T(1,128)} %bitcast.32), calls=%async_computation.1 | async-start | bytes 32768 | tf_op jit(solution)/shard_map/all_to_all | solution.py:72
  182.1 3.5 copy-start.13
  185.6 27.9 %collective-permute-start = (f32[2,256,512]{2,1,0:T(8,128)}, f32[2,256,512]{2,1,0:T(8,128)}, u32[]{:S(2)}, u32[]{:S(2)}) collective-permute-start(f32[2,256,512]{2,1,0:T(8,128)} %get-tuple-element.88), channel_id=1, source_target_pairs={{0,32},{32,64},{64,96},{96,128},{128,160},{160,192},{192,224},{1,3... | collective-permute-start | bytes 3145736 | tf_op jit(solution)/shard_map/while/body/eval_jaxpr/ppermute | solution.py:10
  218.4 27.0 %collective-permute-start = (f32[2,256,512]{2,1,0:T(8,128)}, f32[2,256,512]{2,1,0:T(8,128)}, u32[]{:S(2)}, u32[]{:S(2)}) collective-permute-start(f32[2,256,512]{2,1,0:T(8,128)} %get-tuple-element.88), channel_id=1, source_target_pairs={{0,32},{32,64},{64,96},{96,128},{128,160},{160,192},{192,224},{1,3... | collective-permute-start | bytes 3145736 | tf_op jit(solution)/shard_map/while/body/eval_jaxpr/ppermute | solution.py:10
  250.4 26.2 %collective-permute-start = (f32[2,256,512]{2,1,0:T(8,128)}, f32[2,256,512]{2,1,0:T(8,128)}, u32[]{:S(2)}, u32[]{:S(2)}) collective-permute-start(f32[2,256,512]{2,1,0:T(8,128)} %get-tuple-element.88), channel_id=1, source_target_pairs={{0,32},{32,64},{64,96},{96,128},{128,160},{160,192},{192,224},{1,3... | collective-permute-start | bytes 3145736 | tf_op jit(solution)/shard_map/while/body/eval_jaxpr/ppermute | solution.py:10
  281.6 25.3 %collective-permute-start = (f32[2,256,512]{2,1,0:T(8,128)}, f32[2,256,512]{2,1,0:T(8,128)}, u32[]{:S(2)}, u32[]{:S(2)}) collective-permute-start(f32[2,256,512]{2,1,0:T(8,128)} %get-tuple-element.88), channel_id=1, source_target_pairs={{0,32},{32,64},{64,96},{96,128},{128,160},{160,192},{192,224},{1,3... | collective-permute-start | bytes 3145736 | tf_op jit(solution)/shard_map/while/body/eval_jaxpr/ppermute | solution.py:10
  311.9 24.5 %collective-permute-start = (f32[2,256,512]{2,1,0:T(8,128)}, f32[2,256,512]{2,1,0:T(8,128)}, u32[]{:S(2)}, u32[]{:S(2)}) collective-permute-start(f32[2,256,512]{2,1,0:T(8,128)} %get-tuple-element.88), channel_id=1, source_target_pairs={{0,32},{32,64},{64,96},{96,128},{128,160},{160,192},{192,224},{1,3... | collective-permute-start | bytes 3145736 | tf_op jit(solution)/shard_map/while/body/eval_jaxpr/ppermute | solution.py:10
  341.3 23.6 %collective-permute-start = (f32[2,256,512]{2,1,0:T(8,128)}, f32[2,256,512]{2,1,0:T(8,128)}, u32[]{:S(2)}, u32[]{:S(2)}) collective-permute-start(f32[2,256,512]{2,1,0:T(8,128)} %get-tuple-element.88), channel_id=1, source_target_pairs={{0,32},{32,64},{64,96},{96,128},{128,160},{160,192},{192,224},{1,3... | collective-permute-start | bytes 3145736 | tf_op jit(solution)/shard_map/while/body/eval_jaxpr/ppermute | solution.py:10
  369.9 22.8 %collective-permute-start = (f32[2,256,512]{2,1,0:T(8,128)}, f32[2,256,512]{2,1,0:T(8,128)}, u32[]{:S(2)}, u32[]{:S(2)}) collective-permute-start(f32[2,256,512]{2,1,0:T(8,128)} %get-tuple-element.88), channel_id=1, source_target_pairs={{0,32},{32,64},{64,96},{96,128},{128,160},{160,192},{192,224},{1,3... | collective-permute-start | bytes 3145736 | tf_op jit(solution)/shard_map/while/body/eval_jaxpr/ppermute | solution.py:10
  544.2 9.2 %copy-start.3 = (bf16[1,16,2,128,128]{4,3,1,2,0:T(8,128)(2,1)S(1)}, bf16[1,16,2,128,128]{4,3,1,2,0:T(8,128)(2,1)}, u32[]{:S(2)}) copy-start(bf16[1,16,2,128,128]{4,3,1,2,0:T(8,128)(2,1)} %copy-done.2) | copy-start | bytes 3145732
  553.3 2.4 copy-start.7
  556.5 1.6 copy-start.6
  558.1 1.2 copy-start.5
  561.5 1.6 copy-start.1
where the time goes:
time: 573 us; the launch traced here: 566 us
  waiting for transfers between devices  263 us (46%)
  blocking collectives  108 us (19%)
  matrix products  69.3 us (12%)
  local copies, waits for them, and re-layouts  68.5 us (12%)
  starting transfers between devices  31.3 us (5%)
  other arithmetic  24.5 us (4%)
    ppermute x7, waiting for transfers between devices, passed_along(): return lax.ppermute(x, axis, pairs)  163 us
    all_to_all x1, blocking collectives, body(): lax.all_to_all(slot_rows, 'front', split_axis=1, concat_axis=1, tiled=True)  108 us
    all_to_all x1, waiting for transfers between devices, body(): lax.all_to_all(placed, 'front', split_axis=1, concat_axis=1, tiled=True)  99.9 us
    unnamed x36, local copies, waits for them, and re-layouts  15 us
    ppermute x7, starting transfers between devices, passed_along(): return lax.ppermute(x, axis, pairs)  14.1 us
    reshape x1, local copies, waits for them, and re-layouts, body(): slot_rows = slot_rows.reshape(2, fronts, per_owner, blk, width)  14 us
  transfers between devices with their start and end apart: 9, of which 8 were waited for; matrix products, arithmetic and copies ran while one was open for 1% of the time, Pallas kernels for 0%

commit v1 on v0

--- a/solution.py
+++ b/solution.py
@@ -67,8 +67,14 @@
         "ks,pkbc->psbc", place, partial_value, preferred_element_type=jnp.float32
     ).astype(jnp.bfloat16)
     placed = placed.reshape(2, fronts, per_owner, blk, width)
+    expand_stages_all = lambda x_part: jnp.concatenate(
+        jax.lax.all_to_all(
+            jnp.stack(jnp.split(x_part, jax.lax.axis_size("front"), 1), 0), "front", 0, 0
+        ),
+        1,
+    )
     arrived, arrived_ids = (
-        lax.all_to_all(placed, "front", split_axis=1, concat_axis=1, tiled=True),
+        expand_stages_all(placed),
         lax.all_to_all(slot_ids, "front", split_axis=1, concat_axis=1, tiled=True),
     )
     slot_parts = arrived.reshape(2, slot_total * blk, width)

time: 573 us -> 633 us (1.10)
  local copies, waits for them, and re-layouts: 68.5 us -> 120 us
  matrix products: 69.3 us -> 77.1 us
    unnamed x36 -> x67, local copies, waits for them, and re-layouts: 15 us -> 37.7 us
    split x0 -> x2, local copies, waits for them, and re-layouts: none -> 17.1 us  [body(): jnp.split(x_part, jax.lax.axis_size('front'), 1)]
    all_to_all x1, local copies, waits for them, and re-layouts: 7.62 us -> 14.7 us  [body(): lax.all_to_all(slot_rows, 'front', split_axis=1, concat_axis=1, tiled=True)]
where the time goes in v1:
time: 633 us; the launch traced here: 627 us
  waiting for transfers between devices  263 us (42%)
  local copies, waits for them, and re-layouts  120 us (19%)
  blocking collectives  108 us (17%)
  matrix products  77.1 us (12%)
  starting transfers between devices  31.3 us (5%)
  other arithmetic  25.2 us (4%)
    ppermute x7, waiting for transfers between devices, passed_along(): return lax.ppermute(x, axis, pairs)  163 us
    all_to_all x1, blocking collectives, body(): lax.all_to_all(slot_rows, 'front', split_axis=1, concat_axis=1, tiled=True)  108 us
    all_to_all x1, waiting for transfers between devices, body(): jax.lax.all_to_all(jnp.stack(jnp.split(x_part, jax.lax.axis_size('front')...  99.9 us
    unnamed x67, local copies, waits for them, and re-layouts  37.7 us
    split x2, local copies, waits for them, and re-layouts, body(): jnp.split(x_part, jax.lax.axis_size('front'), 1)  17.1 us
    all_to_all x1, local copies, waits for them, and re-layouts, body(): lax.all_to_all(slot_rows, 'front', split_axis=1, concat_axis=1, tiled=True)  14.7 us
    ppermute x7, starting transfers between devices, passed_along(): return lax.ppermute(x, axis, pairs)  14.1 us
  transfers between devices with their start and end apart: 9, of which 8 were waited for; matrix products, arithmetic and copies ran while one was open for 1% of the time, Pallas kernels for 0%

profile of v1, /device:TPU:129, one launch (start us, length us, event | category | flops | bytes accessed | tf_op | source)
XLA Modules:
  0.0 626.8 jit_solution(15159104053771282709)
XLA Ops:
  0.6 1.4 copy.1263
  2.1 2.8 fusion.26
  8.4 2.8 fusion.47
  11.2 2.3 fusion.34
  13.5 5.1 copy.1171
  18.6 4.4 fusion.35
  23.0 4.5 copy.1172
  27.8 4.7 convert_bitcast_fusion
  32.4 7.1 %fusion.61 = (bf16[2,1,1,128,512]{4,1,3,0,2:T(2,128)(2,1)S(1)}, bf16[2,1,1,128,512]{4,1,3,0,2:T(2,128)(2,1)S(1)}, bf16[2,1,1,128,512]{4,1,3,0,2:T(2,128)(2,1)S(1...) fusion(bf16[2,32,1,128,512]{4,1,3,0,2:T(8,128)(2,1)S(1)} %conve, ...), kind=kLoop, calls=%fused_computation.119 | loop fusion | bytes 6815744 | tf_op jit(solution)/shard_map/split | solution.py:72
  39.5 10.1 %fusion.60 = (bf16[2,1,1,128,512]{4,1,3,0,2:T(2,128)(2,1)S(1)}, bf16[2,1,1,128,512]{4,1,3,0,2:T(2,128)(2,1)S(1)}, bf16[2,1,1,128,512]{4,1,3,0,2:T(2,128)(2,1)S(1...) fusion(bf16[2,32,1,128,512]{4,1,3,0,2:T(8,128)(2,1)S(1)} %conve, ...), kind=kLoop, calls=%fused_computation.118 | loop fusion | bytes 9961472 | tf_op jit(solution)/shard_map/split | solution.py:72
  73.4 8.0 %all-to-all-start = ((bf16[32,2,1,1,128,512]{5,4,1,3,2,0:T(8,128)(2,1)}), bf16[32,2,1,1,128,512]{5,4,1,3,2,0:T(8,128)(2,1)}, u32[]{:S(2)}, u32[]{:S(2)}) async-start(bf16[32,2,1,1,128,512]{5,4,1,3,2,0:T(8,128)(2,1)} %bitcast_dynamic-update-slice_fusion), calls=%async_computation | async-start | bytes 16777216 | tf_op jit(solution)/shard_map/all_to_all | solution.py:71
  82.2 99.9 %all-to-all-done = bf16[32,2,1,1,128,512]{5,4,1,3,2,0:T(8,128)(2,1)} async-done(((bf16[32,2,1,1,128,512]{5,4,1,3,2,0:T(8,128)(2,1)}), bf16[32,2,1,1,128,512]{5,4,1,3,2,0:T(8,128)(2,1)}, u32[]{:S(2)}, u32[]{:S(2)}) %all-to-all-start) | async-done | bytes 8388640 | tf_op jit(solution)/shard_map/all_to_all | solution.py:71
  182.1 9.2 %all-to-all-start.1 = ((s32[1,32,1,128]{3,2,0,1:T(1,128)}), s32[1,32,1,128]{3,2,0,1:T(1,128)S(1)}, u32[]{:S(2)}, u32[]{:S(2)}) async-start(s32[1,32,1,128]{3,2,0,1:T(1,128)} %bitcast.34), calls=%async_computation.1 | async-start | bytes 32768 | tf_op jit(solution)/shard_map/all_to_all | solution.py:78
  191.4 7.6 %copy.1173 = bf16[2,32,1,1,128,512]{5,4,1,0,3,2:T(8,128)(2,1)} copy(bf16[2,32,1,1,128,512]{5,4,0,3,2,1:T(8,128)(2,1)} %bitcast.30) | data formatting | bytes 16777216 | tf_op jit(solution)/shard_map/reshape | solution.py:70
  199.0 6.7 %fusion.39 = f32[2,256,512]{2,1,0:T(8,128)S(1)} fusion(bf16[2,4096,512]{2,1,0:T(8,128)(2,1)} %bitcast.293, s32[4096]{0:T(1024)S(1)} %bitcast.301, bf16[1,2,256,512]{3,2,1,0:T(8,128)(2,1)} %param.15), kind=kOutput, calls=%fused_computation.52 | convolution fusion | flops 2149056512 | bytes 9977856 | tf_op jit(solution)/shard_map/sr,psc->prc/dot_general | solution.py:85
  208.2 1.0 pad_maximum_fusion.1
  209.2 212.0 %while.10 = (s32[]{:T(128)}, f32[2,256,512]{2,1,0:T(8,128)}, f32[1,256]{1,0:T(1,128)S(1)}, f32[2,256,512]{2,1,0:T(8,128)S(1)}, f32[2,2,128,128]{3,2,0,1:T(8,128)S(1)}, /*index=5*/s32[]{:T(128)}) while((s32[]{:T(128)}, f32[2,256,512]{2,1,0:T(8,128)}, f32[1,256]{1,0:T(1,128)S(1)}, f32[2,256,512]{2,1,0:T(8,128)S(1)}, ...), condition=%wide.region_4.5_spmd, body=%wide.region_3.4_spmd.sunk | while | flops 806354944 | bytes 17302636 | solution.py:95
  209.2 2.6 collective-permute-start
  211.9 25.3 %collective-permute-done = f32[2,256,512]{2,1,0:T(8,128)} collective-permute-done((f32[2,256,512]{2,1,0:T(8,128)}, f32[2,256,512]{2,1,0:T(8,128)}, u32[]{:S(2)}, u32[]{:S(2)}) %collective-permute-start) | collective-permute-done | bytes 1048608 | tf_op jit(solution)/shard_map/while/body/eval_jaxpr/ppermute | solution.py:10
  237.1 1.4 multiply_subtract_fusion.2
  241.0 1.0 pad_maximum_fusion.3
  242.1 1.9 collective-permute-start
  244.0 25.1 %collective-permute-done = f32[2,256,512]{2,1,0:T(8,128)} collective-permute-done((f32[2,256,512]{2,1,0:T(8,128)}, f32[2,256,512]{2,1,0:T(8,128)}, u32[]{:S(2)}, u32[]{:S(2)}) %collective-permute-start) | collective-permute-done | bytes 1048608 | tf_op jit(solution)/shard_map/while/body/eval_jaxpr/ppermute | solution.py:10
  269.1 1.4 multiply_subtract_fusion.2
  273.0 1.0 pad_maximum_fusion.3
  274.1 1.9 collective-permute-start
  276.0 24.3 %collective-permute-done = f32[2,256,512]{2,1,0:T(8,128)} collective-permute-done((f32[2,256,512]{2,1,0:T(8,128)}, f32[2,256,512]{2,1,0:T(8,128)}, u32[]{:S(2)}, u32[]{:S(2)}) %collective-permute-start) | collective-permute-done | bytes 1048608 | tf_op jit(solution)/shard_map/while/body/eval_jaxpr/ppermute | solution.py:10
  300.3 1.4 multiply_subtract_fusion.2
  304.2 1.0 pad_maximum_fusion.3
  305.2 1.9 collective-permute-start
  307.1 23.4 %collective-permute-done = f32[2,256,512]{2,1,0:T(8,128)} collective-permute-done((f32[2,256,512]{2,1,0:T(8,128)}, f32[2,256,512]{2,1,0:T(8,128)}, u32[]{:S(2)}, u32[]{:S(2)}) %collective-permute-start) | collective-permute-done | bytes 1048608 | tf_op jit(solution)/shard_map/while/body/eval_jaxpr/ppermute | solution.py:10
  330.6 1.4 multiply_subtract_fusion.2
  334.5 1.0 pad_maximum_fusion.3
  335.5 1.9 collective-permute-start
  337.4 22.6 %collective-permute-done = f32[2,256,512]{2,1,0:T(8,128)} collective-permute-done((f32[2,256,512]{2,1,0:T(8,128)}, f32[2,256,512]{2,1,0:T(8,128)}, u32[]{:S(2)}, u32[]{:S(2)}) %collective-permute-start) | collective-permute-done | bytes 1048608 | tf_op jit(solution)/shard_map/while/body/eval_jaxpr/ppermute | solution.py:10
  360.0 1.4 multiply_subtract_fusion.2
  363.9 1.0 pad_maximum_fusion.3
  364.9 1.9 collective-permute-start
  366.9 21.7 %collective-permute-done = f32[2,256,512]{2,1,0:T(8,128)} collective-permute-done((f32[2,256,512]{2,1,0:T(8,128)}, f32[2,256,512]{2,1,0:T(8,128)}, u32[]{:S(2)}, u32[]{:S(2)}) %collective-permute-start) | collective-permute-done | bytes 1048608 | tf_op jit(solution)/shard_map/while/body/eval_jaxpr/ppermute | solution.py:10
  388.6 1.4 multiply_subtract_fusion.2
  392.5 1.0 pad_maximum_fusion.3
  393.5 1.9 collective-permute-start
  395.4 20.8 %collective-permute-done = f32[2,256,512]{2,1,0:T(8,128)} collective-permute-done((f32[2,256,512]{2,1,0:T(8,128)}, f32[2,256,512]{2,1,0:T(8,128)}, u32[]{:S(2)}, u32[]{:S(2)}) %collective-permute-start) | collective-permute-done | bytes 1048608 | tf_op jit(solution)/shard_map/while/body/eval_jaxpr/ppermute | solution.py:10
  416.3 1.4 multiply_subtract_fusion.2
  420.2 1.0 pad_maximum_fusion.3
  421.2 6.8 %convolution_convert_fusion = bf16[2,512,4096]{2,1,0:T(8,128)(2,1)} fusion(s32[4096]{0:T(1024)S(1)} %bitcast.302, f32[2,256,512]{2,1,0:T(8,128)} %get-tuple-element.29), kind=kOutput, calls=%fused_computation.19 | convolution fusion | flops 2152988672 | bytes 9453568 | tf_op jit(solution)/shard_map/sr,prc->psc/dot_general | solution.py:97
  428.1 9.5 %copy.1226 = bf16[128,8,32,128]{3,2,1,0:T(8,128)(2,1)} copy(bf16[128,8,32,128]{3,1,2,0:T(8,128)(2,1)} %bitcast.271) | data formatting | bytes 16777216
  437.6 9.9 %copy.1178 = bf16[2,32,1,128,512]{3,4,0,2,1:T(8,128)(2,1)} copy(bf16[2,32,1,128,512]{3,1,4,0,2:T(8,128)(2,1)} %bitcast.272) | data formatting | bytes 16777216 | tf_op jit(solution)/shard_map/reshape | solution.py:100
  447.4 108.2 %all_to_all.15 = bf16[2,32,1,128,512]{3,4,0,2,1:T(8,128)(2,1)} all-to-all(bf16[2,32,1,128,512]{3,4,0,2,1:T(8,128)(2,1)} %copy.1178), channel_id=1, replica_groups=mesh['slab'=8,'front'=32] {'front'}, dimensions={1} | all-to-all | bytes 16777216 | tf_op jit(solution)/shard_map/all_to_all | solution.py:101
  555.6 14.7 %copy.1179 = bf16[2,32,1,128,512]{4,1,3,0,2:T(8,128)(2,1)} copy(bf16[2,32,1,128,512]{3,4,0,2,1:T(8,128)(2,1)} %all_to_all.15) | data formatting | bytes 16777216 | tf_op jit(solution)/shard_map/all_to_all | solution.py:101
  570.3 4.7 convert_bitcast_fusion.1
  575.0 2.5 slice_bitcast_fusion.1
  577.4 4.7 copy.1180
  582.1 4.3 fusion.46
  586.4 4.6 copy.1181
  591.0 2.4 fusion.45
  593.4 1.0 copy-done.10
  596.3 1.6 copy-done.6
  598.7 2.7 fusion.43
  601.4 2.7 subtract_bitcast_fusion
  604.1 5.5 copy.1184
  609.6 5.5 add_bitcast_fusion
  615.1 5.4 copy.1185
  620.5 6.0 fusion.10
  (118 shorter events, 51.0 us)
Async XLA Ops:
  0.6 4.2 copy-start.9
  2.1 4.8 copy-start.3
  5.6 1.2 copy-start.11
  6.9 11.7 %copy-start.1 = (bf16[1,16,2,128,128]{4,3,1,2,0:T(8,128)(2,1)}, bf16[1,16,2,128,128]{4,3,1,2,0:T(8,128)(2,1)S(1)}, u32[]{:S(2)}) copy-start(bf16[1,16,2,128,128]{4,3,1,2,0:T(8,128)(2,1)S(1)} %copy.1262) | copy-start | bytes 3145732
  7.6 3.6 copy-start
  23.0 4.5 copy-start.15
  73.4 8.1 %copy-start.14 = (s32[1,16,128]{2,1,0:T(8,128)S(1)}, s32[1,16,128]{2,1,0:T(8,128)}, u32[]{:S(2)}) copy-start(s32[1,16,128]{2,1,0:T(8,128)} %param.14) | copy-start | bytes 24580
  73.4 117.9 %copy-start.12 = (f32[1,2,2,128,128]{4,3,2,1,0:T(8,128)S(1)}, f32[1,2,2,128,128]{4,3,2,1,0:T(8,128)}, u32[]{:S(2)}) copy-start(f32[1,2,2,128,128]{4,3,2,1,0:T(8,128)} %param.16) | copy-start | bytes 786436
  73.4 108.7 %all-to-all-start = ((bf16[32,2,1,1,128,512]{5,4,1,3,2,0:T(8,128)(2,1)}), bf16[32,2,1,1,128,512]{5,4,1,3,2,0:T(8,128)(2,1)}, u32[]{:S(2)}, u32[]{:S(2)}) async-start(bf16[32,2,1,1,128,512]{5,4,1,3,2,0:T(8,128)(2,1)} %bitcast_dynamic-update-slice_fusion), calls=%async_computation | async-start | bytes 16777216 | tf_op jit(solution)/shard_map/all_to_all | solution.py:71
  182.1 16.9 %all-to-all-start.1 = ((s32[1,32,1,128]{3,2,0,1:T(1,128)}), s32[1,32,1,128]{3,2,0,1:T(1,128)S(1)}, u32[]{:S(2)}, u32[]{:S(2)}) async-start(s32[1,32,1,128]{3,2,0,1:T(1,128)} %bitcast.34), calls=%async_computation.1 | async-start | bytes 32768 | tf_op jit(solution)/shard_map/all_to_all | solution.py:78
  205.7 3.5 copy-start.13
  209.2 27.9 %collective-permute-start = (f32[2,256,512]{2,1,0:T(8,128)}, f32[2,256,512]{2,1,0:T(8,128)}, u32[]{:S(2)}, u32[]{:S(2)}) collective-permute-start(f32[2,256,512]{2,1,0:T(8,128)} %get-tuple-element.120), channel_id=1, source_target_pairs={{0,32},{32,64},{64,96},{96,128},{128,160},{160,192},{192,224},{1,3... | collective-permute-start | bytes 3145736 | tf_op jit(solution)/shard_map/while/body/eval_jaxpr/ppermute | solution.py:10
  242.1 27.0 %collective-permute-start = (f32[2,256,512]{2,1,0:T(8,128)}, f32[2,256,512]{2,1,0:T(8,128)}, u32[]{:S(2)}, u32[]{:S(2)}) collective-permute-start(f32[2,256,512]{2,1,0:T(8,128)} %get-tuple-element.120), channel_id=1, source_target_pairs={{0,32},{32,64},{64,96},{96,128},{128,160},{160,192},{192,224},{1,3... | collective-permute-start | bytes 3145736 | tf_op jit(solution)/shard_map/while/body/eval_jaxpr/ppermute | solution.py:10
  274.1 26.2 %collective-permute-start = (f32[2,256,512]{2,1,0:T(8,128)}, f32[2,256,512]{2,1,0:T(8,128)}, u32[]{:S(2)}, u32[]{:S(2)}) collective-permute-start(f32[2,256,512]{2,1,0:T(8,128)} %get-tuple-element.120), channel_id=1, source_target_pairs={{0,32},{32,64},{64,96},{96,128},{128,160},{160,192},{192,224},{1,3... | collective-permute-start | bytes 3145736 | tf_op jit(solution)/shard_map/while/body/eval_jaxpr/ppermute | solution.py:10
  305.2 25.3 %collective-permute-start = (f32[2,256,512]{2,1,0:T(8,128)}, f32[2,256,512]{2,1,0:T(8,128)}, u32[]{:S(2)}, u32[]{:S(2)}) collective-permute-start(f32[2,256,512]{2,1,0:T(8,128)} %get-tuple-element.120), channel_id=1, source_target_pairs={{0,32},{32,64},{64,96},{96,128},{128,160},{160,192},{192,224},{1,3... | collective-permute-start | bytes 3145736 | tf_op jit(solution)/shard_map/while/body/eval_jaxpr/ppermute | solution.py:10
  335.5 24.5 %collective-permute-start = (f32[2,256,512]{2,1,0:T(8,128)}, f32[2,256,512]{2,1,0:T(8,128)}, u32[]{:S(2)}, u32[]{:S(2)}) collective-permute-start(f32[2,256,512]{2,1,0:T(8,128)} %get-tuple-element.120), channel_id=1, source_target_pairs={{0,32},{32,64},{64,96},{96,128},{128,160},{160,192},{192,224},{1,3... | collective-permute-start | bytes 3145736 | tf_op jit(solution)/shard_map/while/body/eval_jaxpr/ppermute | solution.py:10
  364.9 23.6 %collective-permute-start = (f32[2,256,512]{2,1,0:T(8,128)}, f32[2,256,512]{2,1,0:T(8,128)}, u32[]{:S(2)}, u32[]{:S(2)}) collective-permute-start(f32[2,256,512]{2,1,0:T(8,128)} %get-tuple-element.120), channel_id=1, source_target_pairs={{0,32},{32,64},{64,96},{96,128},{128,160},{160,192},{192,224},{1,3... | collective-permute-start | bytes 3145736 | tf_op jit(solution)/shard_map/while/body/eval_jaxpr/ppermute | solution.py:10
  393.5 22.8 %collective-permute-start = (f32[2,256,512]{2,1,0:T(8,128)}, f32[2,256,512]{2,1,0:T(8,128)}, u32[]{:S(2)}, u32[]{:S(2)}) collective-permute-start(f32[2,256,512]{2,1,0:T(8,128)} %get-tuple-element.120), channel_id=1, source_target_pairs={{0,32},{32,64},{64,96},{96,128},{128,160},{160,192},{192,224},{1,3... | collective-permute-start | bytes 3145736 | tf_op jit(solution)/shard_map/while/body/eval_jaxpr/ppermute | solution.py:10
  577.4 4.7 copy-start.2
  591.0 2.4 copy-start.7
  591.0 3.5 copy-start.10
  594.4 1.2 copy-start.4
  595.6 3.1 copy-start.8
  595.6 2.3 copy-start.6
  604.1 5.5 copy-start.5
